TPU v7x, 256 devices: a whole 4x4x8 slice. The times are simulated.
256 devices in a mesh: dp: 32 (over x, y, core), tp: 8 (over z).
Axes of the slice: x: 4, y: 4, z: 8, core: 2. Of those that a mesh axis runs over, the one named last changes fastest.
Arguments:
- arrived_rows: bfloat16 [12288, 7168], P('dp', 'tp'), may hold values from -6 to 6
- row_counts: int32 [32], P('dp'), may hold values from 1 to 384, 4096 in all
- routes: int32 [4096, 8], P('dp'), may hold values from 0 to 31, all different within a row; in each aligned block of 128 rows (0 to 127, 128 to 255, ...) at most 40 rows name the same one
- gate_scale: float32 [4096, 8], P('dp'), may hold values from 0.1 to 0.6
- w_gate: bfloat16 [32, 7168, 1024], P('dp', 'tp'), may hold values from -0.0625 to 0.0625
- w_up: bfloat16 [32, 7168, 1024], P('dp', 'tp'), may hold values from -0.0625 to 0.0625
- w_down: bfloat16 [32, 1024, 7168], P('dp', None, 'tp'), may hold values from -0.1875 to 0.1875
- cotangent: bfloat16 [4096, 7168], P('dp', 'tp'), may hold values from -6 to 6
Outputs:
- layer_out: bfloat16 [4096, 7168], P('dp', 'tp')
- grad_rows: bfloat16 [12288, 7168], P('dp', 'tp')
Inputs may be any that keep to these rules, and one draw needn't show every extreme that they name: `row_counts`: the counts sum to exactly 4096; the largest is exactly 384. `routes`: each row names 8 different experts; within the 128 rows of one index of dp no expert is named by more than 40 rows, a bound that some block reaches.
All inputs are finite; a program needn't handle non-finite values. No bound on the sum of `row_counts` on one device may be relied on, other than what follows from the above.
Results may differ from a plain program's by a relative error of at most 0.03.
Values may be sent and summed in bfloat16 or wider, within the bound.
No kernel may reach another device: no remote copies, remote signals or barrier semaphores. Data moves between devices by JAX's collectives and lax.ppermute only.
A program may use at most 64 MiB of HBM per device.

v0:
```python
import jax
import jax.numpy as jnp
from jax import lax
from jax.sharding import PartitionSpec as P

BF = jnp.bfloat16
F32 = jnp.float32


def rounded(tensor):
    return lax.optimization_barrier(tensor.astype(BF))


def select(left, right):
    return jnp.dot(left, right, preferred_element_type=F32).astype(BF)


def select_t(left, right):
    return lax.dot_general(
        left, right, (((0,), (0,)), ((), ())), preferred_element_type=F32
    ).astype(BF)


def dot_nt(left, right):
    return lax.dot_general(left, right, (((1,), (1,)), ((), ())), preferred_element_type=F32)


def on_device(arrived_rows, row_counts, routes, gate_scale, w_gate, w_up, w_down, cotangent):
    members = lax.axis_size("dp")
    myself = lax.axis_index("dp")
    slot_count, part = arrived_rows.shape
    rows, top = routes.shape
    capacity = rows * top // members + rows * top // (4 * members)
    per_peer = -(-(slot_count // members) // 16) * 16
    gate_proj, up_proj, down_proj = (w_gate[0], w_up[0], w_down[0])

    def exchange(tensor):
        return lax.all_to_all(tensor, "dp", split_axis=0, concat_axis=0, tiled=True)

    ids = jnp.arange(members, dtype=jnp.int32)
    chosen = routes.T[None, :, :] == ids[:, None, None]
    named = jnp.any(chosen, axis=1)
    before = jnp.arange(rows)[:, None] < jnp.arange(rows)[None, :]
    place = jnp.dot(named.astype(BF), before.astype(BF), preferred_element_type=F32)
    place = jnp.where(named, place.astype(jnp.int32), -1)
    slots = jnp.arange(capacity, dtype=jnp.int32)
    hot = place[:, None, :] == slots[None, :, None]
    pack = hot.astype(BF).reshape(members * capacity, rows)
    shipped_grad = exchange(select(pack, cotangent).reshape(members, capacity, part))
    all_counts = lax.all_gather(row_counts, "dp", axis=0, tiled=True)
    starts = jnp.sum(jnp.where(ids[None, :] < ids[:, None], all_counts[None, :], 0), axis=1)
    my_start = starts[myself]
    my_count = all_counts[myself]
    column = jnp.arange(per_peer, dtype=jnp.int32)
    source_slot = (ids[:, None] - my_start) % members + column[None, :] * members
    source_slot = jnp.where(source_slot < my_count, source_slot, -1).reshape(-1)
    spread = (source_slot[:, None] == jnp.arange(slot_count, dtype=jnp.int32)[None, :]).astype(BF)
    incoming = exchange(select(spread, arrived_rows).reshape(members, per_peer, part))
    offset = (jnp.arange(rows, dtype=jnp.int32) * members + myself)[:, None] - starts[None, :]
    held = (offset >= 0) & (offset < all_counts[None, :])
    taken = jnp.where(held, offset // members, -1)
    take = (taken[:, :, None] == column[None, None, :]).astype(BF).reshape(rows, -1)
    balanced = select(take, incoming.reshape(-1, part))
    shipped = exchange(select(pack, balanced).reshape(members, capacity, part))
    grad_part = rounded(dot_nt(shipped_grad.reshape(-1, part), down_proj))
    hidden_grad = lax.psum_scatter(grad_part, "tp", scatter_dimension=0, tiled=True)
    flat = shipped.reshape(-1, part)
    gate_part = rounded(jnp.dot(flat, gate_proj, preferred_element_type=F32))
    up_part = rounded(jnp.dot(flat, up_proj, preferred_element_type=F32))
    gate_pre = lax.psum_scatter(gate_part, "tp", scatter_dimension=0, tiled=True)
    up_pre = lax.psum_scatter(up_part, "tp", scatter_dimension=0, tiled=True)
    gate_pre, up_pre, hidden_grad = (v.astype(F32) for v in (gate_pre, up_pre, hidden_grad))
    sigmoid_gate = jax.nn.sigmoid(gate_pre)
    hidden = (gate_pre * sigmoid_gate * up_pre).astype(BF)
    gate_grad = (
        hidden_grad * up_pre * sigmoid_gate * (1.0 + gate_pre * (1.0 - sigmoid_gate))
    ).astype(BF)
    up_grad = (hidden_grad * gate_pre * sigmoid_gate).astype(BF)
    gate_grad = lax.all_gather(gate_grad, "tp", axis=0, tiled=True)
    up_grad = lax.all_gather(up_grad, "tp", axis=0, tiled=True)
    hidden = lax.all_gather(hidden, "tp", axis=0, tiled=True)
    scale_high = lax.optimization_barrier(gate_scale.astype(BF))
    scale_low = (gate_scale - scale_high.astype(F32)).astype(BF)

    def weights(scale):
        per_expert = jnp.sum(jnp.where(chosen, scale.astype(F32).T[None], 0.0), axis=1)
        return jnp.where(hot, per_expert[:, None, :], 0.0).astype(BF).reshape(-1, rows)

    mix = jnp.concatenate([weights(scale_high), weights(scale_low)], axis=1)

    def combine(returned):
        both = lax.dot_general(
            mix, returned.reshape(-1, part), (((0,), (0,)), ((), ())), preferred_element_type=F32
        )
        return (both[:rows] + both[rows:]).astype(BF)

    input_grad = (dot_nt(gate_grad, gate_proj) + dot_nt(up_grad, up_proj)).astype(BF)
    returned_grad = exchange(input_grad.reshape(members, capacity, part))
    expert_out = jnp.dot(hidden, down_proj, preferred_element_type=F32).astype(BF)
    returned_out = exchange(expert_out.reshape(members, capacity, part))
    balanced_grad = combine(returned_grad)
    leaving = select_t(take, balanced_grad)
    arriving = exchange(leaving.reshape(members, per_peer, part))
    grad_rows = select_t(spread, arriving.reshape(-1, part))
    layer_out = combine(returned_out)
    return (layer_out, grad_rows)


def solution(mesh):
    placed = (
        P("dp", "tp"),
        P("dp"),
        P("dp", None),
        P("dp", None),
        P("dp", "tp", None),
        P("dp", "tp", None),
        P("dp", None, "tp"),
        P("dp", "tp"),
    )
    return jax.shard_map(
        on_device,
        mesh=mesh,
        in_specs=placed,
        out_specs=(P("dp", "tp"), P("dp", "tp")),
        check_vma=False,
    )
```

profile of v0, /device:TPU:1, one launch (start us, length us, event | category | flops | bytes accessed | tf_op | source)
XLA Modules:
  0.0 430.1 jit_solution(9517103195963572123)
XLA Ops:
  7.2 0.0 copy-start
  7.2 0.0 reduce-scatter.8.cloned.1.call-start
  7.2 0.9 fusion.30
  8.1 0.1 fusion.8
  8.2 0.1 eq.80
  8.3 0.2 bitcast_compare_fusion
  8.6 1.7 convolution_convert_fusion.4
  10.3 0.0 copy-start.4
  10.3 39.3 %all_to_all.30 = bf16[32,40,896]{2,1,0:T(8,128)(2,1)S(1)} all-to-all(bf16[32,40,896]{2,1,0:T(8,128)(2,1)S(1)} %bitcast.73), channel_id=1, replica_groups=mesh['dp'=32,'tp'=8] {'dp'}, dimensions={0} | all-to-all | bytes 4587520 | tf_op jit(solution)/shard_map/all_to_all | solution.py:38
  49.6 4.3 convolution_convert_fusion
  53.9 0.0 reduce-scatter.8.cloned.1.call-update
  54.6 0.6 dynamic-slice
  55.2 0.8 dynamic-update-slice
  56.0 10.0 %all-reduce = s32[32]{0:T(128)S(1)} all-reduce(s32[32]{0:T(128)S(1)} %dynamic-update-slice), channel_id=1, replica_groups=mesh['dp'=32,'tp'=8] {'dp'}, use_global_device_ids=true, to_apply=%add | all-reduce | flops 32 | bytes 256
  66.0 0.6 dynamic_slice.7
  66.6 0.1 select_reduce_fusion.2
  66.7 0.6 dynamic_slice.6
  67.3 0.7 and_select_fusion
  68.0 0.1 broadcast_add_fusion
  68.1 0.1 add.78
  68.1 0.7 compare_select_fusion
  68.8 1.6 convolution_convert_fusion.7
  70.4 8.7 %all-to-all-start = ((bf16[32,16,896]{2,1,0:T(8,128)(2,1)}), bf16[32,16,896]{2,1,0:T(8,128)(2,1)S(1)}, u32[]{:S(2)}, u32[]{:S(2)}) async-start(bf16[32,16,896]{2,1,0:T(8,128)(2,1)} %bitcast.80), calls=%async_computation | async-start | bytes 1835008 | tf_op jit(solution)/shard_map/all_to_all | solution.py:38
  79.1 0.0 reduce-scatter.4.cloned.1.call-start
  79.2 0.1 fusion.32
  79.3 15.3 %all-to-all-done = bf16[32,16,896]{2,1,0:T(8,128)(2,1)S(1)} async-done(((bf16[32,16,896]{2,1,0:T(8,128)(2,1)}), bf16[32,16,896]{2,1,0:T(8,128)(2,1)S(1)}, u32[]{:S(2)}, u32[]{:S(2)}) %all-to-all-start) | async-done | bytes 917536 | tf_op jit(solution)/shard_map/all_to_all | solution.py:38
  94.6 2.5 convolution_convert_fusion.5
  97.1 34.8 %all_to_all.31 = bf16[32,40,896]{2,1,0:T(8,128)(2,1)S(1)} all-to-all(bf16[32,40,896]{2,1,0:T(8,128)(2,1)} %bitcast.72), channel_id=1, replica_groups=mesh['dp'=32,'tp'=8] {'dp'}, dimensions={0} | all-to-all | bytes 4587520 | tf_op jit(solution)/shard_map/all_to_all | solution.py:38
  131.9 1.4 copy-done.1
  133.3 4.1 convolution_convert_fusion.2
  137.4 0.0 reduce-scatter.4.cloned.1.call-update
  137.5 0.0 reduce-scatter.6.cloned.1.call-start
  137.5 6.6 %convolution_convert_fusion.1 = bf16[1280,1024]{1,0:T(8,128)(2,1)} fusion(bf16[1280,896]{1,0:T(8,128)(2,1)} %bitcast.76, bf16[1,896,1024]{2,1,0:T(8,128)(2,1)} %param.13), kind=kOutput, calls=%fused_computation.2 | convolution fusion | flops 2350120960 | bytes 6750208 | tf_op jit(solution)/shard_map/dot_general | solution.py:69
  144.1 0.0 reduce-scatter.6.cloned.1.call-update
  144.1 0.0 all-gather.6.cloned.1.call-start
  144.1 0.0 reduce-scatter.8.cloned.1.call-done
  144.2 32.4 %reduce-scatter.4.cloned.1.call-done = bf16[160,1024]{1,0:T(8,128)(2,1)} async-done(((bf16[1280,1024]{1,0:T(8,128)(2,1)}), bf16[160,1024]{1,0:T(8,128)(2,1)}) %reduce-scatter.4.cloned.1.call-update) | async-done | bytes 327696 | tf_op jit(solution)/shard_map/reduce_scatter | solution.py:70
  176.5 46.1 %reduce-scatter.6.cloned.1.call-done = bf16[160,1024]{1,0:T(8,128)(2,1)} async-done(((bf16[1280,1024]{1,0:T(8,128)(2,1)}), bf16[160,1024]{1,0:T(8,128)(2,1)}) %reduce-scatter.6.cloned.1.call-update) | async-done | bytes 327696 | tf_op jit(solution)/shard_map/reduce_scatter | solution.py:71
  222.6 2.5 fusion.18
  225.2 0.0 all-gather.6.cloned.1.call-update
  225.2 0.0 all-gather.8.cloned.1.call-start
  225.3 0.5 all-gather.8.cloned.1.call-update
  225.8 0.2 all-gather.4.cloned.1.call-start
  226.0 0.3 all-gather.4.cloned.1.call-update
  226.4 41.7 %all-gather.6.cloned.1.call-done = bf16[1280,1024]{1,0:T(8,128)(2,1)} async-done(((bf16[160,1024]{1,0:T(8,128)(2,1)}), bf16[1280,1024]{1,0:T(8,128)(2,1)}) %all-gather.6.cloned.1.call-update) | async-done | bytes 2621456 | tf_op jit(solution)/shard_map/all_gather | solution.py:79
  268.1 6.7 %fusion.4 = f32[1280,896]{1,0:T(8,128)} fusion(bf16[1280,1024]{1,0:T(8,128)(2,1)} %all-gather.6.cloned.1.call-done, bf16[1,896,1024]{2,1,0:T(8,128)(2,1)S(1)} %copy-done), kind=kOutput, calls=%fused_computation.11 | convolution fusion | flops 2348810240 | bytes 9043968 | tf_op jit(solution)/shard_map/dot_general | solution.py:25
  274.8 36.4 %all-gather.8.cloned.1.call-done = bf16[1280,1024]{1,0:T(8,128)(2,1)} async-done(((bf16[160,1024]{1,0:T(8,128)(2,1)}), bf16[1280,1024]{1,0:T(8,128)(2,1)}) %all-gather.8.cloned.1.call-update) | async-done | bytes 2621456 | tf_op jit(solution)/shard_map/all_gather | solution.py:80
  311.3 7.9 %add_convert_fusion = bf16[1280,896]{1,0:T(8,128)(2,1)} fusion(f32[1280,896]{1,0:T(8,128)} %fusion.4, bf16[1280,1024]{1,0:T(8,128)(2,1)} %all-gather.8.cloned.1.call-done, bf16[1,896,1024]{2,1,0:T(8,128)(2,1)} %param.13), kind=kOutput, calls=%fused_computation | convolution fusion | flops 2351104000 | bytes 11337728 | tf_op jit(solution)/shard_map/dot_general | solution.py:25
  319.2 10.5 %all-to-all-start.4 = ((bf16[32,40,896]{2,1,0:T(8,128)(2,1)}), bf16[32,40,896]{2,1,0:T(8,128)(2,1)}, u32[]{:S(2)}, u32[]{:S(2)}) async-start(bf16[32,40,896]{2,1,0:T(8,128)(2,1)} %bitcast.77), calls=%async_computation.7 | async-start | bytes 4587520 | tf_op jit(solution)/shard_map/all_to_all | solution.py:38
  329.7 24.2 %all-gather.4.cloned.1.call-done = bf16[1280,1024]{1,0:T(8,128)(2,1)} async-done(((bf16[160,1024]{1,0:T(8,128)(2,1)}), bf16[1280,1024]{1,0:T(8,128)(2,1)}) %all-gather.4.cloned.1.call-update) | async-done | bytes 2621456 | tf_op jit(solution)/shard_map/all_gather | solution.py:81
  353.9 6.6 %convolution_convert_fusion.3 = bf16[1280,896]{1,0:T(8,128)(2,1)} fusion(bf16[1280,1024]{1,0:T(8,128)(2,1)} %all-gather.4.cloned.1.call-done, bf16[1,1024,896]{2,1,0:T(8,128)(2,1)} %param.14), kind=kOutput, calls=%fused_computation.4 | convolution fusion | flops 2349957120 | bytes 6750208 | tf_op jit(solution)/shard_map/dot_general | solution.py:99
  360.5 10.7 %all-to-all-start.2 = ((bf16[32,40,896]{2,1,0:T(8,128)(2,1)}), bf16[32,40,896]{2,1,0:T(8,128)(2,1)}, u32[]{:S(2)}, u32[]{:S(2)}) async-start(bf16[32,40,896]{2,1,0:T(8,128)(2,1)} %bitcast.74), calls=%async_computation.4 | async-start | bytes 4587520 | tf_op jit(solution)/shard_map/all_to_all | solution.py:38
  371.2 0.1 eq.91
  371.3 0.1 bitcast_compare_fusion.1
  371.4 0.1 select_reduce_fusion.1
  371.5 0.2 fusion.20
  371.8 2.5 fusion.23
  374.3 1.4 convolution_convert_fusion.6
  375.7 26.0 %all-to-all-done.2 = bf16[32,40,896]{2,1,0:T(8,128)(2,1)} async-done(((bf16[32,40,896]{2,1,0:T(8,128)(2,1)}), bf16[32,40,896]{2,1,0:T(8,128)(2,1)}, u32[]{:S(2)}, u32[]{:S(2)}) %all-to-all-start.2) | async-done | bytes 2293792 | tf_op jit(solution)/shard_map/all_to_all | solution.py:38
  401.6 4.5 %all-to-all-start.5 = ((bf16[32,16,896]{2,1,0:T(8,128)(2,1)}), bf16[32,16,896]{2,1,0:T(8,128)(2,1)S(1)}, u32[]{:S(2)}, u32[]{:S(2)}) async-start(bf16[32,16,896]{2,1,0:T(8,128)(2,1)} %bitcast.23), calls=%async_computation.8 | async-start | bytes 1835008 | tf_op jit(solution)/shard_map/all_to_all | solution.py:38
  406.1 2.5 fusion.24
  408.6 0.7 fusion.22
  409.4 12.3 %all-to-all-done.5 = bf16[32,16,896]{2,1,0:T(8,128)(2,1)S(1)} async-done(((bf16[32,16,896]{2,1,0:T(8,128)(2,1)}), bf16[32,16,896]{2,1,0:T(8,128)(2,1)S(1)}, u32[]{:S(2)}, u32[]{:S(2)}) %all-to-all-start.5) | async-done | bytes 917536 | tf_op jit(solution)/shard_map/all_to_all | solution.py:38
  421.7 1.5 convolution_convert_fusion.8
  (20 shorter events, 0.1 us)
Async XLA Ops:
  7.2 126.1 %copy-start = (bf16[1,896,1024]{2,1,0:T(8,128)(2,1)S(1)}, bf16[1,896,1024]{2,1,0:T(8,128)(2,1)}, u32[]{:S(2)}) copy-start(bf16[1,896,1024]{2,1,0:T(8,128)(2,1)} %param.12) | copy-start | bytes 5505028
  7.2 137.0 %reduce-scatter.8.cloned.1.call-start = ((), (), s32[]{:S(2)}) async-start(), calls=%async_computation.12 | async-start | bytes 2949120 | tf_op jit(solution)/shard_map/reduce_scatter | solution.py:66
  10.3 39.3 %copy-start.4 = (bf16[1,1024,896]{2,1,0:T(8,128)(2,1)S(1)}, bf16[1,1024,896]{2,1,0:T(8,128)(2,1)}, u32[]{:S(2)}) copy-start(bf16[1,1024,896]{2,1,0:T(8,128)(2,1)} %param.14) | copy-start | bytes 5505028
  53.9 0.7 copy-start.6
  53.9 14.9 %copy-start.5 = (bf16[384,896]{1,0:T(8,128)(2,1)S(1)}, bf16[384,896]{1,0:T(8,128)(2,1)}, u32[]{:S(2)}) copy-start(bf16[384,896]{1,0:T(8,128)(2,1)} %param.8) | copy-start | bytes 2064388
  70.4 24.2 %all-to-all-start = ((bf16[32,16,896]{2,1,0:T(8,128)(2,1)}), bf16[32,16,896]{2,1,0:T(8,128)(2,1)S(1)}, u32[]{:S(2)}, u32[]{:S(2)}) async-start(bf16[32,16,896]{2,1,0:T(8,128)(2,1)} %bitcast.80), calls=%async_computation | async-start | bytes 1835008 | tf_op jit(solution)/shard_map/all_to_all | solution.py:38
  79.1 97.4 %reduce-scatter.4.cloned.1.call-start = ((), (), s32[]{:S(2)}) async-start(), calls=%async_computation.9 | async-start | bytes 2949120 | tf_op jit(solution)/shard_map/reduce_scatter | solution.py:70
  131.9 1.4 copy-start.1
  137.5 85.2 %reduce-scatter.6.cloned.1.call-start = ((), (), s32[]{:S(2)}) async-start(), calls=%async_computation.10 | async-start | bytes 2949120 | tf_op jit(solution)/shard_map/reduce_scatter | solution.py:71
  144.1 124.0 %all-gather.6.cloned.1.call-start = ((), (), s32[]{:S(2)}) async-start(), calls=%async_computation.13 | async-start | bytes 2949120 | tf_op jit(solution)/shard_map/all_gather | solution.py:79
  225.2 86.0 %all-gather.8.cloned.1.call-start = ((), (), s32[]{:S(2)}) async-start(), calls=%async_computation.14 | async-start | bytes 2949120 | tf_op jit(solution)/shard_map/all_gather | solution.py:80
  225.8 128.1 %all-gather.4.cloned.1.call-start = ((), (), s32[]{:S(2)}) async-start(), calls=%async_computation.11 | async-start | bytes 2949120 | tf_op jit(solution)/shard_map/all_gather | solution.py:81
  319.2 41.3 %all-to-all-start.4 = ((bf16[32,40,896]{2,1,0:T(8,128)(2,1)}), bf16[32,40,896]{2,1,0:T(8,128)(2,1)}, u32[]{:S(2)}, u32[]{:S(2)}) async-start(bf16[32,40,896]{2,1,0:T(8,128)(2,1)} %bitcast.77), calls=%async_computation.7 | async-start | bytes 4587520 | tf_op jit(solution)/shard_map/all_to_all | solution.py:38
  360.5 10.7 %copy-start.3 = (f32[128,8]{0,1:T(8,128)S(1)}, f32[128,8]{0,1:T(8,128)}, u32[]{:S(2)}) copy-start(f32[128,8]{0,1:T(8,128)} %param.11) | copy-start | bytes 12292
  360.5 11.0 %copy-start.2 = (s32[128,8]{0,1:T(8,128)S(1)}, s32[128,8]{0,1:T(8,128)}, u32[]{:S(2)}) copy-start(s32[128,8]{0,1:T(8,128)} %param.10) | copy-start | bytes 12292
  360.5 41.1 %all-to-all-start.2 = ((bf16[32,40,896]{2,1,0:T(8,128)(2,1)}), bf16[32,40,896]{2,1,0:T(8,128)(2,1)}, u32[]{:S(2)}, u32[]{:S(2)}) async-start(bf16[32,40,896]{2,1,0:T(8,128)(2,1)} %bitcast.74), calls=%async_computation.4 | async-start | bytes 4587520 | tf_op jit(solution)/shard_map/all_to_all | solution.py:38
  401.6 20.1 %all-to-all-start.5 = ((bf16[32,16,896]{2,1,0:T(8,128)(2,1)}), bf16[32,16,896]{2,1,0:T(8,128)(2,1)S(1)}, u32[]{:S(2)}, u32[]{:S(2)}) async-start(bf16[32,16,896]{2,1,0:T(8,128)(2,1)} %bitcast.23), calls=%async_computation.8 | async-start | bytes 1835008 | tf_op jit(solution)/shard_map/all_to_all | solution.py:38
Sparse Core Ops, SparseCore 0:
  54.0 39.0 reduce-scatter.7
  137.6 38.9 reduce-scatter.3
  179.1 43.4 reduce-scatter.5
  225.3 42.7 all-gather.5
  270.3 40.9 all-gather.7
  312.9 40.9 all-gather.3
where the time goes:
time: 431 us; the launch traced here: 430 us
  waiting for transfers between devices  235 us (55%)
  blocking collectives  84.1 us (20%)
  matrix products  50.1 us (12%)
  starting transfers between devices  34.8 us (8%)
  between operations  15 us (3%)
  other arithmetic  6.42 us (1%)
    all_to_all x2, blocking collectives, exchange(): return lax.all_to_all(tensor, 'dp', split_axis=0, concat_axis=0, tiled=True)  74.1 us
    all_to_all x4, waiting for transfers between devices, exchange(): return lax.all_to_all(tensor, 'dp', split_axis=0, concat_axis=0, tiled=True)  53.6 us
    reduce_scatter x1, waiting for transfers between devices, on_device(): up_pre = lax.psum_scatter(up_part, 'tp', scatter_dimension=0, tiled=True)  46.1 us
    all_gather x1, waiting for transfers between devices, on_device(): gate_grad = lax.all_gather(gate_grad, 'tp', axis=0, tiled=True)  41.7 us
    all_gather x1, waiting for transfers between devices, on_device(): up_grad = lax.all_gather(up_grad, 'tp', axis=0, tiled=True)  36.4 us
    all_to_all x4, starting transfers between devices, exchange(): return lax.all_to_all(tensor, 'dp', split_axis=0, concat_axis=0, tiled=True)  34.3 us
    reduce_scatter x1, waiting for transfers between devices, on_device(): lax.psum_scatter(gate_part, 'tp', scatter_dimension=0, tiled=True)  32.4 us
    all_gather x1, waiting for transfers between devices, on_device(): hidden = lax.all_gather(hidden, 'tp', axis=0, tiled=True)  24.2 us
  transfers between devices with their start and end apart: 10, of which 8 were waited for; matrix products, arithmetic and copies ran while one was open for 11% of the time, Pallas kernels for 0%

commit v1 on v0

--- a/solution.py
+++ b/solution.py
@@ -78,7 +78,9 @@
     up_grad = (hidden_grad * gate_pre * sigmoid_gate).astype(BF)
     gate_grad = lax.all_gather(gate_grad, "tp", axis=0, tiled=True)
     up_grad = lax.all_gather(up_grad, "tp", axis=0, tiled=True)
-    hidden = lax.all_gather(hidden, "tp", axis=0, tiled=True)
+    hidden = jnp.concatenate(
+        lax.all_to_all(jnp.stack([hidden] * lax.axis_size("tp")), "tp", 0, 0), axis=0
+    )
     scale_high = lax.optimization_barrier(gate_scale.astype(BF))
     scale_low = (gate_scale - scale_high.astype(F32)).astype(BF)
 

time: 431 us -> 473 us (1.097)
  waiting for transfers between devices: 235 us -> 276 us
    all_gather x1, waiting for transfers between devices: 41.7 us -> 81.3 us  [on_device(): gate_grad = lax.all_gather(gate_grad, 'tp', axis=0, tiled=True)]
    all_gather x1 -> x0, waiting for transfers between devices: 24.2 us -> none  [on_device(): hidden = lax.all_gather(hidden, 'tp', axis=0, tiled=True)]
    all_to_all x4, waiting for transfers between devices: 53.6 us -> 77.7 us  [exchange(): return lax.all_to_all(tensor, 'dp', split_axis=0, concat_axis=0, tiled=True)]
    all_to_all x0 -> x1, starting transfers between devices: none -> 5.46 us  [on_device(): lax.all_to_all(jnp.stack([hidden] * lax.axis_size('tp')), 'tp', 0, 0)]
    all_to_all x4, starting transfers between devices: 34.3 us -> 29.1 us  [exchange(): return lax.all_to_all(tensor, 'dp', split_axis=0, concat_axis=0, tiled=True)]
where the time goes in v1:
time: 473 us; the launch traced here: 472 us
  waiting for transfers between devices  276 us (58%)
  blocking collectives  84.2 us (18%)
  matrix products  50.1 us (11%)
  starting transfers between devices  34.8 us (7%)
  between operations  14.7 us (3%)
  other arithmetic  6.33 us (1%)
  local copies, waits for them, and re-layouts  6.15 us (1%)
    all_gather x1, waiting for transfers between devices, on_device(): gate_grad = lax.all_gather(gate_grad, 'tp', axis=0, tiled=True)  81.3 us
    all_to_all x4, waiting for transfers between devices, exchange(): return lax.all_to_all(tensor, 'dp', split_axis=0, concat_axis=0, tiled=True)  77.7 us
    all_to_all x2, blocking collectives, exchange(): return lax.all_to_all(tensor, 'dp', split_axis=0, concat_axis=0, tiled=True)  74.1 us
    reduce_scatter x1, waiting for transfers between devices, on_device(): up_pre = lax.psum_scatter(up_part, 'tp', scatter_dimension=0, tiled=True)  46 us
    all_gather x1, waiting for transfers between devices, on_device(): up_grad = lax.all_gather(up_grad, 'tp', axis=0, tiled=True)  37.7 us
    reduce_scatter x1, waiting for transfers between devices, on_device(): lax.psum_scatter(gate_part, 'tp', scatter_dimension=0, tiled=True)  32.3 us
    all_to_all x4, starting transfers between devices, exchange(): return lax.all_to_all(tensor, 'dp', split_axis=0, concat_axis=0, tiled=True)  29.1 us
    dot_general x3, matrix products, dot_nt(): lax.dot_general(left, right, (((1,), (1,)), ((), ())), preferred_element_...  19 us
  transfers between devices with their start and end apart: 10, of which 8 were waited for; matrix products, arithmetic and copies ran while one was open for 11% of the time, Pallas kernels for 0%

profile of v1, /device:TPU:1, one launch (start us, length us, event | category | flops | bytes accessed | tf_op | source)
XLA Modules:
  0.0 471.8 jit_solution(12392538902849432737)
XLA Ops:
  7.2 0.0 copy-start
  7.2 0.0 reduce-scatter.8.cloned.1.call-start
  7.2 0.9 fusion.30
  8.1 0.1 fusion.8
  8.2 0.1 eq.80
  8.3 0.2 bitcast_compare_fusion
  8.6 1.7 convolution_convert_fusion.4
  10.3 0.0 copy-start.4
  10.3 39.3 %all_to_all.35 = bf16[32,40,896]{2,1,0:T(8,128)(2,1)S(1)} all-to-all(bf16[32,40,896]{2,1,0:T(8,128)(2,1)S(1)} %bitcast.74), channel_id=1, replica_groups=mesh['dp'=32,'tp'=8] {'dp'}, dimensions={0} | all-to-all | bytes 4587520 | tf_op jit(solution)/shard_map/all_to_all | solution.py:38
  49.6 4.3 convolution_convert_fusion
  53.9 0.0 reduce-scatter.8.cloned.1.call-update
  54.6 0.6 dynamic-slice
  55.2 0.8 dynamic-update-slice
  56.0 10.0 %all-reduce = s32[32]{0:T(128)S(1)} all-reduce(s32[32]{0:T(128)S(1)} %dynamic-update-slice), channel_id=1, replica_groups=mesh['dp'=32,'tp'=8] {'dp'}, use_global_device_ids=true, to_apply=%add | all-reduce | flops 32 | bytes 256
  66.0 0.6 dynamic_slice.7
  66.6 0.1 select_reduce_fusion.2
  66.7 0.6 dynamic_slice.6
  67.3 0.7 and_select_fusion
  68.0 0.1 broadcast_add_fusion
  68.0 0.1 add.78
  68.1 0.7 compare_select_fusion
  68.8 1.7 convolution_convert_fusion.7
  70.4 8.7 %all-to-all-start = ((bf16[32,16,896]{2,1,0:T(8,128)(2,1)}), bf16[32,16,896]{2,1,0:T(8,128)(2,1)S(1)}, u32[]{:S(2)}, u32[]{:S(2)}) async-start(bf16[32,16,896]{2,1,0:T(8,128)(2,1)} %bitcast.81), calls=%async_computation | async-start | bytes 1835008 | tf_op jit(solution)/shard_map/all_to_all | solution.py:38
  79.1 0.0 reduce-scatter.4.cloned.1.call-start
  79.2 0.1 fusion.32
  79.3 15.3 %all-to-all-done = bf16[32,16,896]{2,1,0:T(8,128)(2,1)S(1)} async-done(((bf16[32,16,896]{2,1,0:T(8,128)(2,1)}), bf16[32,16,896]{2,1,0:T(8,128)(2,1)S(1)}, u32[]{:S(2)}, u32[]{:S(2)}) %all-to-all-start) | async-done | bytes 917536 | tf_op jit(solution)/shard_map/all_to_all | solution.py:38
  94.6 2.5 convolution_convert_fusion.5
  97.1 34.8 %all_to_all.36 = bf16[32,40,896]{2,1,0:T(8,128)(2,1)S(1)} all-to-all(bf16[32,40,896]{2,1,0:T(8,128)(2,1)} %bitcast.73), channel_id=1, replica_groups=mesh['dp'=32,'tp'=8] {'dp'}, dimensions={0} | all-to-all | bytes 4587520 | tf_op jit(solution)/shard_map/all_to_all | solution.py:38
  131.9 1.4 copy-done.1
  133.3 4.1 convolution_convert_fusion.2
  137.5 0.0 reduce-scatter.4.cloned.1.call-update
  137.5 0.0 reduce-scatter.6.cloned.1.call-start
  137.5 6.6 %convolution_convert_fusion.1 = bf16[1280,1024]{1,0:T(8,128)(2,1)} fusion(bf16[1280,896]{1,0:T(8,128)(2,1)} %bitcast.78, bf16[1,896,1024]{2,1,0:T(8,128)(2,1)} %param.13), kind=kOutput, calls=%fused_computation.2 | convolution fusion | flops 2350120960 | bytes 6750208 | tf_op jit(solution)/shard_map/dot_general | solution.py:69
  144.1 0.0 reduce-scatter.6.cloned.1.call-update
  144.1 0.0 all-gather.3.cloned.1.call-start
  144.2 0.0 reduce-scatter.8.cloned.1.call-done
  144.2 32.3 %reduce-scatter.4.cloned.1.call-done = bf16[160,1024]{1,0:T(8,128)(2,1)} async-done(((bf16[1280,1024]{1,0:T(8,128)(2,1)}), bf16[160,1024]{1,0:T(8,128)(2,1)}) %reduce-scatter.4.cloned.1.call-update) | async-done | bytes 327696 | tf_op jit(solution)/shard_map/reduce_scatter | solution.py:70
  176.5 46.0 %reduce-scatter.6.cloned.1.call-done = bf16[160,1024]{1,0:T(8,128)(2,1)} async-done(((bf16[1280,1024]{1,0:T(8,128)(2,1)}), bf16[160,1024]{1,0:T(8,128)(2,1)}) %reduce-scatter.6.cloned.1.call-update) | async-done | bytes 327696 | tf_op jit(solution)/shard_map/reduce_scatter | solution.py:71
  222.5 2.5 fusion.18
  224.9 0.0 all-gather.3.cloned.1.call-update
  225.0 0.0 all-gather.5.cloned.1.call-start
  225.0 0.5 all-gather.5.cloned.1.call-update
  225.5 1.9 stack.2
  227.4 5.5 %all-to-all-start.2 = ((bf16[8,160,1024]{2,1,0:T(8,128)(2,1)}), bf16[8,160,1024]{2,1,0:T(8,128)(2,1)}, u32[]{:S(2)}, u32[]{:S(2)}) async-start(bf16[8,160,1024]{2,1,0:T(8,128)(2,1)} %stack.2), calls=%async_computation.4 | async-start | bytes 5242880 | tf_op jit(solution)/shard_map/all_to_all | solution.py:82
  232.9 81.3 %all-gather.3.cloned.1.call-done = bf16[1280,1024]{1,0:T(8,128)(2,1)} async-done(((bf16[160,1024]{1,0:T(8,128)(2,1)}), bf16[1280,1024]{1,0:T(8,128)(2,1)}) %all-gather.3.cloned.1.call-update) | async-done | bytes 2621456 | tf_op jit(solution)/shard_map/all_gather | solution.py:79
  314.2 6.7 %fusion.4 = f32[1280,896]{1,0:T(8,128)} fusion(bf16[1280,1024]{1,0:T(8,128)(2,1)} %all-gather.3.cloned.1.call-done, bf16[1,896,1024]{2,1,0:T(8,128)(2,1)S(1)} %copy-done), kind=kOutput, calls=%fused_computation.11 | convolution fusion | flops 2348810240 | bytes 9043968 | tf_op jit(solution)/shard_map/dot_general | solution.py:25
  320.9 37.7 %all-gather.5.cloned.1.call-done = bf16[1280,1024]{1,0:T(8,128)(2,1)} async-done(((bf16[160,1024]{1,0:T(8,128)(2,1)}), bf16[1280,1024]{1,0:T(8,128)(2,1)}) %all-gather.5.cloned.1.call-update) | async-done | bytes 2621456 | tf_op jit(solution)/shard_map/all_gather | solution.py:80
  358.7 8.0 %add_convert_fusion = bf16[1280,896]{1,0:T(8,128)(2,1)} fusion(f32[1280,896]{1,0:T(8,128)} %fusion.4, bf16[1280,1024]{1,0:T(8,128)(2,1)} %all-gather.5.cloned.1.call-done, bf16[1,896,1024]{2,1,0:T(8,128)(2,1)} %param.13), kind=kOutput, calls=%fused_computation | convolution fusion | flops 2351104000 | bytes 11337728 | tf_op jit(solution)/shard_map/dot_general | solution.py:25
  366.6 10.5 %all-to-all-start.5 = ((bf16[32,40,896]{2,1,0:T(8,128)(2,1)}), bf16[32,40,896]{2,1,0:T(8,128)(2,1)}, u32[]{:S(2)}, u32[]{:S(2)}) async-start(bf16[32,40,896]{2,1,0:T(8,128)(2,1)} %bitcast.76), calls=%async_computation.8 | async-start | bytes 4587520 | tf_op jit(solution)/shard_map/all_to_all | solution.py:38
  377.2 6.6 %convolution_convert_fusion.3 = bf16[1280,896]{1,0:T(8,128)(2,1)} fusion(bf16[1280,1024]{1,0:T(8,128)(2,1)} %bitcast.15, bf16[1,1024,896]{2,1,0:T(8,128)(2,1)} %param.14), kind=kOutput, calls=%fused_computation.4 | convolution fusion | flops 2349957120 | bytes 6750208 | tf_op jit(solution)/shard_map/dot_general | solution.py:101
  383.7 23.9 %all-to-all-done.5 = bf16[32,40,896]{2,1,0:T(8,128)(2,1)} async-done(((bf16[32,40,896]{2,1,0:T(8,128)(2,1)}), bf16[32,40,896]{2,1,0:T(8,128)(2,1)}, u32[]{:S(2)}, u32[]{:S(2)}) %all-to-all-start.5) | async-done | bytes 2293792 | tf_op jit(solution)/shard_map/all_to_all | solution.py:38
  407.7 5.4 %all-to-all-start.3 = ((bf16[32,40,896]{2,1,0:T(8,128)(2,1)}), bf16[32,40,896]{2,1,0:T(8,128)(2,1)}, u32[]{:S(2)}, u32[]{:S(2)}) async-start(bf16[32,40,896]{2,1,0:T(8,128)(2,1)} %bitcast.75), calls=%async_computation.5 | async-start | bytes 4587520 | tf_op jit(solution)/shard_map/all_to_all | solution.py:38
  413.1 0.1 eq.91
  413.2 0.1 bitcast_compare_fusion.1
  413.4 0.1 select_reduce_fusion.1
  413.5 0.2 fusion.20
  413.7 2.5 fusion.23
  416.2 1.3 convolution_convert_fusion.6
  417.6 26.1 %all-to-all-done.3 = bf16[32,40,896]{2,1,0:T(8,128)(2,1)} async-done(((bf16[32,40,896]{2,1,0:T(8,128)(2,1)}), bf16[32,40,896]{2,1,0:T(8,128)(2,1)}, u32[]{:S(2)}, u32[]{:S(2)}) %all-to-all-start.3) | async-done | bytes 2293792 | tf_op jit(solution)/shard_map/all_to_all | solution.py:38
  443.7 4.5 all-to-all-start.6
  448.2 2.5 fusion.24
  450.7 0.7 fusion.22
  451.4 12.3 %all-to-all-done.6 = bf16[32,16,896]{2,1,0:T(8,128)(2,1)S(1)} async-done(((bf16[32,16,896]{2,1,0:T(8,128)(2,1)}), bf16[32,16,896]{2,1,0:T(8,128)(2,1)S(1)}, u32[]{:S(2)}, u32[]{:S(2)}) %all-to-all-start.6) | async-done | bytes 917536 | tf_op jit(solution)/shard_map/all_to_all | solution.py:38
  463.7 1.5 convolution_convert_fusion.8
  (20 shorter events, 0.1 us)
Async XLA Ops:
  7.2 126.2 %copy-start = (bf16[1,896,1024]{2,1,0:T(8,128)(2,1)S(1)}, bf16[1,896,1024]{2,1,0:T(8,128)(2,1)}, u32[]{:S(2)}) copy-start(bf16[1,896,1024]{2,1,0:T(8,128)(2,1)} %param.12) | copy-start | bytes 5505028
  7.2 137.0 %reduce-scatter.8.cloned.1.call-start = ((), (), s32[]{:S(2)}) async-start(), calls=%async_computation.12 | async-start | bytes 2949120 | tf_op jit(solution)/shard_map/reduce_scatter | solution.py:66
  10.3 39.3 %copy-start.4 = (bf16[1,1024,896]{2,1,0:T(8,128)(2,1)S(1)}, bf16[1,1024,896]{2,1,0:T(8,128)(2,1)}, u32[]{:S(2)}) copy-start(bf16[1,1024,896]{2,1,0:T(8,128)(2,1)} %param.14) | copy-start | bytes 5505028
  53.9 0.7 copy-start.6
  53.9 14.9 %copy-start.5 = (bf16[384,896]{1,0:T(8,128)(2,1)S(1)}, bf16[384,896]{1,0:T(8,128)(2,1)}, u32[]{:S(2)}) copy-start(bf16[384,896]{1,0:T(8,128)(2,1)} %param.8) | copy-start | bytes 2064388
  70.4 24.2 %all-to-all-start = ((bf16[32,16,896]{2,1,0:T(8,128)(2,1)}), bf16[32,16,896]{2,1,0:T(8,128)(2,1)S(1)}, u32[]{:S(2)}, u32[]{:S(2)}) async-start(bf16[32,16,896]{2,1,0:T(8,128)(2,1)} %bitcast.81), calls=%async_computation | async-start | bytes 1835008 | tf_op jit(solution)/shard_map/all_to_all | solution.py:38
  79.1 97.4 %reduce-scatter.4.cloned.1.call-start = ((), (), s32[]{:S(2)}) async-start(), calls=%async_computation.10 | async-start | bytes 2949120 | tf_op jit(solution)/shard_map/reduce_scatter | solution.py:70
  131.9 1.5 copy-start.1
  137.5 85.0 %reduce-scatter.6.cloned.1.call-start = ((), (), s32[]{:S(2)}) async-start(), calls=%async_computation.11 | async-start | bytes 2949120 | tf_op jit(solution)/shard_map/reduce_scatter | solution.py:71
  144.1 170.1 %all-gather.3.cloned.1.call-start = ((), (), s32[]{:S(2)}) async-start(), calls=%async_computation.13 | async-start | bytes 2949120 | tf_op jit(solution)/shard_map/all_gather | solution.py:79
  225.0 133.7 %all-gather.5.cloned.1.call-start = ((), (), s32[]{:S(2)}) async-start(), calls=%async_computation.14 | async-start | bytes 2949120 | tf_op jit(solution)/shard_map/all_gather | solution.py:80
  227.4 139.2 %all-to-all-start.2 = ((bf16[8,160,1024]{2,1,0:T(8,128)(2,1)}), bf16[8,160,1024]{2,1,0:T(8,128)(2,1)}, u32[]{:S(2)}, u32[]{:S(2)}) async-start(bf16[8,160,1024]{2,1,0:T(8,128)(2,1)} %stack.2), calls=%async_computation.4 | async-start | bytes 5242880 | tf_op jit(solution)/shard_map/all_to_all | solution.py:82
  366.6 41.0 %all-to-all-start.5 = ((bf16[32,40,896]{2,1,0:T(8,128)(2,1)}), bf16[32,40,896]{2,1,0:T(8,128)(2,1)}, u32[]{:S(2)}, u32[]{:S(2)}) async-start(bf16[32,40,896]{2,1,0:T(8,128)(2,1)} %bitcast.76), calls=%async_computation.8 | async-start | bytes 4587520 | tf_op jit(solution)/shard_map/all_to_all | solution.py:38
  407.7 5.4 %copy-start.3 = (f32[128,8]{0,1:T(8,128)S(1)}, f32[128,8]{0,1:T(8,128)}, u32[]{:S(2)}) copy-start(f32[128,8]{0,1:T(8,128)} %param.11) | copy-start | bytes 12292
  407.7 5.7 %copy-start.2 = (s32[128,8]{0,1:T(8,128)S(1)}, s32[128,8]{0,1:T(8,128)}, u32[]{:S(2)}) copy-start(s32[128,8]{0,1:T(8,128)} %param.10) | copy-start | bytes 12292
  407.7 36.0 %all-to-all-start.3 = ((bf16[32,40,896]{2,1,0:T(8,128)(2,1)}), bf16[32,40,896]{2,1,0:T(8,128)(2,1)}, u32[]{:S(2)}, u32[]{:S(2)}) async-start(bf16[32,40,896]{2,1,0:T(8,128)(2,1)} %bitcast.75), calls=%async_computation.5 | async-start | bytes 4587520 | tf_op jit(solution)/shard_map/all_to_all | solution.py:38
  443.7 20.1 %all-to-all-start.6 = ((bf16[32,16,896]{2,1,0:T(8,128)(2,1)}), bf16[32,16,896]{2,1,0:T(8,128)(2,1)S(1)}, u32[]{:S(2)}, u32[]{:S(2)}) async-start(bf16[32,16,896]{2,1,0:T(8,128)(2,1)} %bitcast.24), calls=%async_computation.9 | async-start | bytes 1835008 | tf_op jit(solution)/shard_map/all_to_all | solution.py:38
Sparse Core Ops, SparseCore 0:
  54.0 39.0 reduce-scatter.7
  137.6 38.8 reduce-scatter.3
  179.1 43.3 reduce-scatter.5
  225.1 89.0 all-gather.2
  316.4 42.2 all-gather.4
